TPU v7x, 32 devices: a whole 2x2x4 slice. The times are simulated.
32 devices in a mesh: dp: 4 (over z), ctx: 8 (over y, x, core).
Axes of the slice: x: 2, y: 2, z: 4, core: 2. Of those that a mesh axis runs over, the one named last changes fastest.
Arguments:
- tokens: bfloat16 [4096, 1152], P(('dp', 'ctx')), may hold values from -6 to 6
- in_gain: bfloat16 [1152], P('dp'), may hold values from 0.099609375 to 1.8984375
- query_weight: bfloat16 [1152, 1024], P('dp'), may hold values from -0.1875 to 0.1875
- key_weight: bfloat16 [1152, 256], P('dp'), may hold values from -0.1875 to 0.1875
- value_weight: bfloat16 [1152, 256], P('dp'), may hold values from -0.1875 to 0.1875
- query_gain: bfloat16 [256], P('dp'), may hold values from 0.099609375 to 1.8984375
- key_gain: bfloat16 [256], P('dp'), may hold values from 0.099609375 to 1.8984375
- out_weight: bfloat16 [1024, 1152], P('dp'), may hold values from -0.75 to 0.75
- attn_post_gain: bfloat16 [1152], P('dp'), may hold values from 0.099609375 to 1.8984375
- ffn_pre_gain: bfloat16 [1152], P('dp'), may hold values from 0.099609375 to 1.8984375
- gate_weight: bfloat16 [1152, 6912], P('dp', 'ctx'), may hold values from -0.1875 to 0.1875
- up_weight: bfloat16 [1152, 6912], P('dp', 'ctx'), may hold values from -0.1875 to 0.1875
- down_weight: bfloat16 [1152, 6912], P('dp', 'ctx'), may hold values from -0.078125 to 0.078125
- ffn_post_gain: bfloat16 [1152], P('dp'), may hold values from 0.099609375 to 1.8984375
- cotangent: bfloat16 [4096, 1152], P(('dp', 'ctx')), may hold values from -6 to 6
Outputs:
- block_out: bfloat16 [4096, 1152], P(('dp', 'ctx'))
- input_grad: float32 [4096, 1152], P(('dp', 'ctx'))
- in_gain_grad: float32 [1152], P('dp')
- query_weight_grad: float32 [1152, 1024], P('dp')
- key_weight_grad: float32 [1152, 256], P('dp')
- value_weight_grad: float32 [1152, 256], P('dp')
- query_gain_grad: float32 [256], P('dp')
- key_gain_grad: float32 [256], P('dp')
- out_weight_grad: float32 [1024, 1152], P('dp')
- attn_post_gain_grad: float32 [1152], P('dp')
- ffn_pre_gain_grad: float32 [1152], P('dp')
- gate_weight_grad: float32 [1152, 6912], P('dp', 'ctx')
- up_weight_grad: float32 [1152, 6912], P('dp', 'ctx')
- down_weight_grad: float32 [1152, 6912], P('dp', 'ctx')
- ffn_post_gain_grad: float32 [1152], P('dp')
All inputs are finite; a program needn't handle non-finite values.
Results may differ from a plain program's by a relative error of at most 0.017.
Values may be sent and summed in bfloat16 or wider, within the bound.
A program may use at most 128 MiB of HBM per device.

v0:
```python
import functools
import math

import jax
import jax.numpy as jnp
from jax import lax
from jax.experimental import pallas as pl
from jax.experimental.layout import Layout, with_layout_constraint
from jax.experimental.pallas import tpu as pltpu
from jax.sharding import PartitionSpec as P

HEADS = 4
HEAD = 256


EPS = 1e-06
GELU_C = math.sqrt(2.0 / math.pi)
NEG_FILL = -1e30


def inverse_rms(values):
    return lax.rsqrt(jnp.mean(values * values, axis=-1, keepdims=True) + EPS)


def norm_back(values, scale_inv, gain, grad_out):
    weighted = grad_out * gain
    cubed = scale_inv * scale_inv * scale_inv
    return scale_inv * weighted - values * cubed * jnp.mean(
        weighted * values, axis=-1, keepdims=True
    )


def gelu_pair(values):
    inner = GELU_C * (values + 0.044715 * values * values * values)
    tanh_val = jnp.tanh(inner)
    result = 0.5 * values * (1.0 + tanh_val)
    slope = 0.5 * (1.0 + tanh_val) + 0.5 * values * (1.0 - tanh_val * tanh_val) * GELU_C * (
        1.0 + 3.0 * 0.044715 * values * values
    )
    return (result, slope)


def rotate(values, cosine, sine):
    middle = values.shape[-1] // 2
    first = values[..., :middle]
    second = values[..., middle:]
    return jnp.concatenate(
        [first * cosine - second * sine, second * cosine + first * sine], axis=-1
    )


def unrotate(grads, cosine, sine):
    middle = grads.shape[-1] // 2
    first = grads[..., :middle]
    second = grads[..., middle:]
    return jnp.concatenate(
        [first * cosine + second * sine, second * cosine - first * sine], axis=-1
    )


def rope_tables(positions):
    middle = HEAD // 2
    freqs = jnp.exp(-(2.0 * jnp.arange(middle, dtype=jnp.float32) / HEAD) * math.log(1000000.0))
    angles = positions[:, None] * freqs[None, :]
    return (jnp.cos(angles), jnp.sin(angles))


def matmul(left, right):
    return jnp.dot(left, right, preferred_element_type=jnp.float32)


def matmul_tn(left, right):
    return lax.dot_general(
        left, right, (((0,), (0,)), ((), ())), preferred_element_type=jnp.float32
    )


def matmul_nt(left, right):
    return lax.dot_general(
        left, right, (((1,), (1,)), ((), ())), preferred_element_type=jnp.float32
    )


MESH = pl.DeviceIdType.MESH


def swap_kernel(size, axis, kinds, *refs):
    count = len(kinds)
    ins, outs, kept = refs[:count], refs[count : 2 * count], refs[2 * count : 3 * count]
    send, recv, local = refs[3 * count :]
    me = lax.axis_index(axis)
    own = []
    for item, kind in enumerate(kinds):
        source = ins[item].at[me] if kind == "swap" else ins[item]
        own.append(pltpu.make_async_copy(source, kept[item], local.at[item, 0]))
        own[-1].start()
    barrier = pltpu.get_barrier_semaphore()
    for step in range(1, size):
        peer = lax.rem(me + step, size)
        pl.semaphore_signal(barrier, inc=1, device_id={axis: peer}, device_id_type=MESH)
    pl.semaphore_wait(barrier, size - 1)
    copies = []
    for item, kind in enumerate(kinds):
        for step in range(1, size):
            peer = lax.rem(me + step, size)
            source = ins[item].at[peer] if kind == "swap" else ins[item]
            copy = pltpu.make_async_remote_copy(
                src_ref=source,
                dst_ref=outs[item].at[me],
                send_sem=send.at[item, step - 1],
                recv_sem=recv.at[item, step - 1],
                device_id={axis: peer},
                device_id_type=MESH,
            )
            copy.start()
            copies.append(copy)
    for item in range(count):
        own[item].wait()
        copy = pltpu.make_async_copy(kept[item], outs[item].at[me], local.at[item, 1])
        copy.start()
        copies.append(copy)
    for copy in copies:
        copy.wait()


def chunks_of(rows):
    for parts in (4, 3, 2):
        if rows % (16 * parts) == 0:
            return parts
    return 1


def pair_gather_kernel(size, axis, kinds, *refs):
    count = len(kinds)
    ins, outs, kept = refs[:count], refs[count : 2 * count], refs[2 * count : 3 * count]
    send, recv, pass_send, pass_recv, local = refs[3 * count :]
    me = lax.axis_index(axis)
    twin = me + 1 - 2 * lax.rem(me, 2)
    half = size // 2
    own = []
    for item in range(count):
        own.append(pltpu.make_async_copy(ins[item], kept[item], local.at[item, 0]))
        own[-1].start()
    barrier = pltpu.get_barrier_semaphore()
    for step in range(1, half):
        peer = lax.rem(me + 2 * step, size)
        pl.semaphore_signal(barrier, inc=1, device_id={axis: peer}, device_id_type=MESH)
    pl.semaphore_signal(barrier, inc=1, device_id={axis: twin}, device_id_type=MESH)
    pl.semaphore_wait(barrier, half)
    pieces = []
    for item in range(count):
        rows = ins[item].shape[0]
        pieces += [
            (item, part, pl.ds(part * (rows // chunks_of(rows)), rows // chunks_of(rows)))
            for part in range(chunks_of(rows))
        ]
    across, last = [], []
    for item, part, span in pieces:
        for step in range(1, half):
            copy = pltpu.make_async_remote_copy(
                src_ref=ins[item].at[span],
                dst_ref=outs[item].at[me, span],
                send_sem=send.at[item, step, part],
                recv_sem=recv.at[item, step, part],
                device_id={axis: lax.rem(me + 2 * step, size)},
                device_id_type=MESH,
            )
            copy.start()
            across.append((copy, item, step, part, span))
    for item, part, span in pieces:
        copy = pltpu.make_async_remote_copy(
            src_ref=ins[item].at[span],
            dst_ref=outs[item].at[me, span],
            send_sem=pass_send.at[item, 0, part],
            recv_sem=pass_recv.at[item, 0, part],
            device_id={axis: twin},
            device_id_type=MESH,
        )
        copy.start()
        last.append(copy)
    for item in range(count):
        own[item].wait()
        copy = pltpu.make_async_copy(kept[item], outs[item].at[me], local.at[item, 1])
        copy.start()
        last.append(copy)
    for arrived, item, step, part, span in across:
        arrived.wait_recv()
        origin = lax.rem(me + size - 2 * step, size)
        copy = pltpu.make_async_remote_copy(
            src_ref=outs[item].at[origin, span],
            dst_ref=outs[item].at[origin, span],
            send_sem=pass_send.at[item, step, part],
            recv_sem=pass_recv.at[item, step, part],
            device_id={axis: twin},
            device_id_type=MESH,
        )
        copy.start()
        last.append(copy)
    for sent, *_ in across:
        sent.wait_send()
    for copy in last:
        copy.wait()


def exchange(arrays, kinds, axis, size, ident):
    count = len(arrays)
    pairs = all(kind == "gather" for kind in kinds) and axis == "ctx" and size % 2 == 0
    shapes = tuple(
        jax.ShapeDtypeStruct(x.shape if kind == "swap" else (size,) + x.shape, x.dtype)
        for x, kind in zip(arrays, kinds)
    )
    dma = pltpu.SemaphoreType.DMA
    if pairs:
        half = size // 2
        parts = max(chunks_of(x.shape[0]) for x in arrays)
        scratch = [dma((count, half, parts))] * 4
        body = pair_gather_kernel
    else:
        scratch = [dma((count, size - 1))] * 2
        body = swap_kernel
    moved = sum(x.size * x.dtype.itemsize for x in shapes)
    return pl.pallas_call(
        functools.partial(body, size, axis, tuple(kinds)),
        out_shape=shapes,
        in_specs=[pl.BlockSpec(memory_space=pl.ANY)] * count,
        out_specs=tuple(pl.BlockSpec(memory_space=pl.ANY) for _ in arrays),
        scratch_shapes=[pltpu.VMEM(x.shape[1:], x.dtype) for x in shapes]
        + scratch
        + [dma((count, 2))],
        compiler_params=pltpu.CompilerParams(collective_id=ident, has_side_effects=True),
        cost_estimate=pl.CostEstimate(flops=0, bytes_accessed=20 * moved, transcendentals=0),
        name=f"exchange_{ident}",
    )(*arrays)


def pieces_of(rows):
    parts = chunks_of(rows)
    return [pl.ds(part * (rows // parts), rows // parts) for part in range(parts)]


def remote(source, target, send, recv, axis, peer):
    copy = pltpu.make_async_remote_copy(
        src_ref=source,
        dst_ref=target,
        send_sem=send,
        recv_sem=recv,
        device_id={axis: peer},
        device_id_type=MESH,
    )
    copy.start()
    return copy


class Place:
    def __init__(self, axis, size):
        self.axis, self.size, self.half = axis, size, size // 2
        self.me = lax.axis_index(axis)
        self.core = lax.rem(self.me, 2)
        self.twin = self.me + 1 - 2 * self.core

    def across(self, step):
        return lax.rem(self.me + 2 * step, self.size)

    def behind(self, step):
        return lax.rem(self.me + self.size - 2 * step, self.size)

    def greet_pairs(self):
        barrier = pltpu.get_barrier_semaphore()
        for step in range(1, self.half):
            pl.semaphore_signal(
                barrier, inc=1, device_id={self.axis: self.across(step)}, device_id_type=MESH
            )
        pl.semaphore_signal(barrier, inc=1, device_id={self.axis: self.twin}, device_id_type=MESH)
        pl.semaphore_wait(barrier, self.half)

    def greet_all(self):
        barrier = pltpu.get_barrier_semaphore()
        for step in range(1, self.size):
            peer = lax.rem(self.me + step, self.size)
            pl.semaphore_signal(barrier, inc=1, device_id={self.axis: peer}, device_id_type=MESH)
        pl.semaphore_wait(barrier, self.size - 1)


def scatter_scratch(size, rows, width):
    half, parts, dma = size // 2, chunks_of(rows), pltpu.SemaphoreType.DMA
    block = lambda count: pltpu.VMEM((count, rows, width), jnp.bfloat16)
    return [block(half), block(half), block(half - 1), block(half - 1), dma((half,))] + [
        dma((half, parts))
    ] * 4


class Scatter:
    def __init__(self, place, part, scratch):
        self.place, self.part = place, part
        self.kept, self.twins, self.summed, self.landed = scratch[:4]
        self.local, self.twin_send, self.twin_recv, self.send, self.recv = scratch[4:]
        self.spans = pieces_of(self.kept.shape[1])

    def load(self):
        place = self.place
        self.loads = []
        for slot in range(place.half):
            copy = pltpu.make_async_copy(
                self.part.at[place.across(slot)], self.kept.at[slot], self.local.at[slot]
            )
            copy.start()
            self.loads.append(copy)

    def start(self):
        place = self.place
        self.twin_copies, self.copies = {}, {}
        slots = list(range(1, place.half)) + [0]
        for index, span in enumerate(self.spans):
            for slot in slots:
                self.twin_copies[slot, index] = remote(
                    self.part.at[place.across(slot) + 1 - 2 * place.core, span],
                    self.twins.at[slot, span],
                    self.twin_send.at[slot, index],
                    self.twin_recv.at[slot, index],
                    place.axis,
                    place.twin,
                )
        for copy in self.loads:
            copy.wait()
        for index, span in enumerate(self.spans):
            for slot in slots[:-1]:
                self.twin_copies[slot, index].wait_recv()
                self.summed[slot - 1, span] = (
                    self.kept[slot, span].astype(jnp.float32)
                    + self.twins[slot, span].astype(jnp.float32)
                ).astype(jnp.bfloat16)
                self.copies[slot, index] = remote(
                    self.summed.at[slot - 1, span],
                    self.landed.at[slot - 1, span],
                    self.send.at[slot, index],
                    self.recv.at[slot, index],
                    place.axis,
                    place.across(slot),
                )

    def total(self, index):
        span = self.spans[index]
        self.twin_copies[0, index].wait_recv()
        value = self.kept[0, span].astype(jnp.float32) + self.twins[0, span].astype(jnp.float32)
        for slot in range(1, self.place.half):
            self.copies[slot, index].wait_recv()
            value = value + self.landed[slot - 1, span].astype(jnp.float32)
        return value

    def finish(self):
        for copy in list(self.twin_copies.values()) + list(self.copies.values()):
            copy.wait_send()


def gather_scratch(size, rows):
    dma = pltpu.SemaphoreType.DMA
    return [dma((size // 2, chunks_of(rows)))] * 4 + [dma((chunks_of(rows),))]


class Gather:
    def __init__(self, place, source, target, scratch):
        self.place, self.source, self.target = place, source, target
        self.send, self.recv, self.pass_send, self.pass_recv, self.local = scratch
        self.spans = pieces_of(source.shape[0])
        self.across, self.last = [], []

    def start(self, index):
        place, span = self.place, self.spans[index]
        for step in range(1, place.half):
            copy = remote(
                self.source.at[span],
                self.target.at[place.me, span],
                self.send.at[step, index],
                self.recv.at[step, index],
                place.axis,
                place.across(step),
            )
            self.across.append((copy, step, index))
        self.last.append(
            remote(
                self.source.at[span],
                self.target.at[place.me, span],
                self.pass_send.at[0, index],
                self.pass_recv.at[0, index],
                place.axis,
                place.twin,
            )
        )
        copy = pltpu.make_async_copy(
            self.source.at[span], self.target.at[place.me, span], self.local.at[index]
        )
        copy.start()
        self.last.append(copy)

    def relay(self):
        place = self.place
        for copy, step, index in self.across:
            copy.wait_recv()
            block = self.target.at[place.behind(step), self.spans[index]]
            self.last.append(
                remote(
                    block,
                    block,
                    self.pass_send.at[step, index],
                    self.pass_recv.at[step, index],
                    place.axis,
                    place.twin,
                )
            )

    def finish(self):
        for copy, *_ in self.across:
            copy.wait_send()
        for copy in self.last:
            copy.wait()


def ffn_turn_kernel(axis, size, part, residual, cot, gain, block_out, gain_grad, gathered, grad, *scratch):
    place = Place(axis, size)
    scatter = Scatter(place, part, scratch[:9])
    gather = Gather(place, grad, gathered, scratch[9:])
    scatter.load()
    place.greet_pairs()
    scatter.start()
    gain_row = gain[...]
    for index, span in enumerate(scatter.spans):
        ffn_sum = scatter.total(index)
        inverse = inverse_rms(ffn_sum)
        incoming = cot[span].astype(jnp.float32)
        grad[span] = norm_back(ffn_sum, inverse, gain_row, incoming).astype(jnp.bfloat16)
        gather.start(index)
        scaled = ffn_sum * inverse
        block_out[span] = (residual[span] + scaled * gain_row).astype(jnp.bfloat16)
        share = jnp.sum(incoming * scaled, axis=0, keepdims=True)
        gain_grad[...] = share if index == 0 else gain_grad[...] + share
    gather.relay()
    scatter.finish()
    gather.finish()


def ffn_turn(part, residual, cotangent, gain, axis, size, ident):
    rows, width = residual.shape
    whole = pl.BlockSpec(memory_space=pltpu.VMEM)
    away = pl.BlockSpec(memory_space=pl.ANY)
    return pl.pallas_call(
        functools.partial(ffn_turn_kernel, axis, size),
        out_shape=(
            jax.ShapeDtypeStruct((rows, width), jnp.bfloat16),
            jax.ShapeDtypeStruct((1, width), jnp.float32),
            jax.ShapeDtypeStruct((size, rows, width), jnp.bfloat16),
        ),
        in_specs=[away, whole, whole, whole],
        out_specs=(whole, whole, away),
        scratch_shapes=[pltpu.VMEM((rows, width), jnp.bfloat16)]
        + scatter_scratch(size, rows, width)
        + gather_scratch(size, rows),
        compiler_params=pltpu.CompilerParams(collective_id=ident, has_side_effects=True),
        cost_estimate=pl.CostEstimate(
            flops=0, bytes_accessed=20 * part.size * 2, transcendentals=0
        ),
        name=f"ffn_turn_{ident}",
    )(part, residual, cotangent, gain)


def attn_back_kernel(
    axis,
    size,
    part,
    residual,
    cot,
    projected,
    tokens,
    gains,
    out_hbm,
    query_hbm,
    pair_hbm,
    attn_out,
    query_rot,
    key_hbm,
    value_hbm,
    queries,
    keys,
    cosine,
    sine,
    post_grad,
    input_grad,
    query_cols,
    pair_cols,
    proj_cols,
    all_gains,
    out_w,
    query_w,
    pair_w,
    key_all,
    value_all,
    res_grad,
    proj_grad,
    stacked_p,
    stacked_s,
    stacked_g,
    stacked_q,
    pair_part,
    query_grad,
    query_send,
    pair_send,
    proj_send,
    gain_send,
    local,
    send,
    recv,
    *scratch,
):
    rows, width = residual.shape
    total_keys = key_all.shape[0]
    bf16, f32 = jnp.bfloat16, jnp.float32
    scaling = 1.0 / math.sqrt(HEAD)
    place = Place(axis, size)
    me = place.me
    two = Scatter(place, part, scratch[:9])
    pairs = Scatter(place, pair_part, scratch[9:])
    two.load()
    loads = []
    for source, target in (
        (out_hbm, out_w),
        (key_hbm, key_all),
        (value_hbm, value_all),
        (query_hbm, query_w),
        (pair_hbm, pair_w),
    ):
        copy = pltpu.make_async_copy(source, target, local.at[len(loads)])
        copy.start()
        loads.append(copy)
    place.greet_all()
    two.start()
    swaps = []

    def swap(item, source, target):
        for step in range(1, size):
            peer = lax.rem(me + step, size)
            swaps.append(
                remote(
                    source.at[peer],
                    target.at[me],
                    send.at[item, step - 1],
                    recv.at[item, step - 1],
                    axis,
                    peer,
                )
            )
        copy = pltpu.make_async_copy(source.at[me], target.at[me], local.at[len(loads) + item])
        copy.start()
        swaps.append(copy)

    gain_in, gain_attn, gain_pre = gains[0:1], gains[1:2], gains[2:3]
    gain_query, gain_key = gains[4:5, :HEAD], gains[4:5, HEAD : 2 * HEAD]
    here = pl.ds(pl.multiple_of(me * rows, rows), rows)
    cos_here, sin_here = cosine[here], sine[here]
    gain_send[...] = jnp.zeros_like(gain_send)
    gain_send[3:4] = post_grad[...]
    proj_width = width // size
    for index, span in enumerate(two.spans):
        two_grad = two.total(index)
        kept = residual[span]
        inv_two = inverse_rms(kept)
        back = cot[span].astype(f32) + norm_back(kept, inv_two, gain_pre, two_grad)
        res_grad[span] = back
        ahead = projected[span]
        inv_proj = inverse_rms(ahead)
        proj_back = norm_back(ahead, inv_proj, gain_attn, back)
        proj_grad[span] = proj_back.astype(bf16)
        for peer in range(size):
            proj_send[peer, span] = proj_back[:, peer * proj_width : (peer + 1) * proj_width].astype(
                bf16
            )
        gain_send[2:3] += jnp.sum(two_grad * kept * inv_two, axis=0, keepdims=True)
        gain_send[1:2] += jnp.sum(back * ahead * inv_proj, axis=0, keepdims=True)
    swap(0, proj_send, proj_cols)
    loads[0].wait()
    query_grad[...] = matmul_nt(proj_grad[...], out_w[...]).astype(bf16)
    loads[1].wait()
    loads[2].wait()

    def probabilities(head, carry):
        lanes = pl.ds(pl.multiple_of(head * HEAD, HEAD), HEAD)
        level = pl.ds(pl.multiple_of(head * rows, rows), rows)
        query_pos = me * rows + lax.broadcasted_iota(jnp.int32, (rows, total_keys), 0)
        allowed = query_pos >= lax.broadcasted_iota(jnp.int32, (rows, total_keys), 1)
        query = query_rot[:, lanes]
        incoming = query_grad[:, lanes]
        scores = jnp.where(allowed, matmul_nt(query, key_all[...]), NEG_FILL)
        weights = jnp.where(
            allowed, jnp.exp(scores - jnp.max(scores, axis=-1, keepdims=True)), 0.0
        )
        probs = weights / jnp.sum(weights, axis=-1, keepdims=True)
        delta = jnp.sum(
            incoming.astype(f32) * attn_out[:, lanes].astype(f32), axis=-1, keepdims=True
        )
        prob_grad = matmul_nt(incoming, value_all[...])
        stacked_s[level] = (probs * (prob_grad - delta)).astype(bf16)
        stacked_p[level] = probs.astype(bf16)
        stacked_g[level] = incoming
        stacked_q[level] = query
        return carry

    lax.fori_loop(0, HEADS, probabilities, 0)
    values_part = matmul_tn(stacked_p[...], stacked_g[...]).astype(bf16)
    keys_part = matmul_tn(stacked_s[...], stacked_q[...]).astype(bf16)
    for peer in range(size):
        block = slice(peer * rows, (peer + 1) * rows)
        pair_part[peer, :, :HEAD] = keys_part[block]
        pair_part[peer, :, HEAD:] = values_part[block]
    pairs.load()
    pairs.start()
    query_width = HEADS * HEAD // size

    def query_back(head, share):
        lanes = pl.ds(pl.multiple_of(head * HEAD, HEAD), HEAD)
        level = pl.ds(pl.multiple_of(head * rows, rows), rows)
        normed_grad = unrotate(
            matmul(stacked_s[level], key_all[...]) * scaling, cosine[here], sine[here]
        )
        value = queries[:, lanes]
        inverse = inverse_rms(value)
        query_grad[:, lanes] = norm_back(value, inverse, gain_query, normed_grad).astype(bf16)
        return share + jnp.sum(normed_grad * value * inverse, axis=0, keepdims=True)

    gain_share = lax.fori_loop(0, HEADS, query_back, jnp.zeros((1, HEAD), f32))
    for peer in range(size):
        query_send[peer] = query_grad[:, peer * query_width : (peer + 1) * query_width]
    swap(1, query_send, query_cols)
    gain_send[4:5, :HEAD] = gain_share
    loads[3].wait()
    input_grad[...] = matmul_nt(query_grad[...], query_w[...])
    loads[4].wait()
    pair_width = 2 * HEAD // size
    key_share = jnp.zeros((1, HEAD), f32)
    for index, span in enumerate(pairs.spans):
        pair_total = pairs.total(index)
        near = slice(span.start, span.start + span.size)
        normed_grad = unrotate(pair_total[:, :HEAD], cos_here[near], sin_here[near])
        value = keys[span]
        inverse = inverse_rms(value)
        key_share = key_share + jnp.sum(normed_grad * value * inverse, axis=0, keepdims=True)
        both = jnp.concatenate(
            [norm_back(value, inverse, gain_key, normed_grad), pair_total[:, HEAD:]], axis=1
        )
        for peer in range(size):
            pair_send[peer, span] = both[:, peer * pair_width : (peer + 1) * pair_width].astype(bf16)
        one_grad = input_grad[span] + matmul_nt(both.astype(bf16), pair_w[...])
        inputs = tokens[span].astype(f32)
        inv_one = inverse_rms(inputs)
        gain_send[0:1] += jnp.sum(one_grad * inputs * inv_one, axis=0, keepdims=True)
        input_grad[span] = res_grad[span] + norm_back(inputs, inv_one, gain_in, one_grad)
    gain_send[5:6, :HEAD] = key_share
    swap(2, pair_send, pair_cols)
    for step in range(1, size):
        peer = lax.rem(me + step, size)
        swaps.append(
            remote(
                gain_send,
                all_gains.at[me],
                send.at[3, step - 1],
                recv.at[3, step - 1],
                axis,
                peer,
            )
        )
    copy = pltpu.make_async_copy(gain_send, all_gains.at[me], local.at[len(loads) + 3])
    copy.start()
    swaps.append(copy)
    two.finish()
    pairs.finish()
    for copy in swaps:
        copy.wait()


def attn_back(
    part,
    residual,
    cotangent,
    projected,
    tokens,
    gains,
    out_full,
    query_full,
    pair_full,
    attn_out,
    query_rot,
    key_all,
    value_all,
    queries,
    keys,
    cosine,
    sine,
    post_grad,
    axis,
    size,
    ident,
):
    rows, width = residual.shape
    bf16, f32 = jnp.bfloat16, jnp.float32
    whole = pl.BlockSpec(memory_space=pltpu.VMEM)
    away = pl.BlockSpec(memory_space=pl.ANY)
    qwidth, total_keys = query_full.shape[1], key_all.shape[0]
    query_cols = (size, rows, qwidth // size)
    pair_cols = (size, rows, 2 * HEAD // size)
    proj_cols = (size, rows, width // size)
    dma = pltpu.SemaphoreType.DMA
    return pl.pallas_call(
        functools.partial(attn_back_kernel, axis, size),
        out_shape=(
            jax.ShapeDtypeStruct((rows, width), f32),
            jax.ShapeDtypeStruct(query_cols, bf16),
            jax.ShapeDtypeStruct(pair_cols, bf16),
            jax.ShapeDtypeStruct(proj_cols, bf16),
            jax.ShapeDtypeStruct((size, 8, width), f32),
        ),
        in_specs=[away]
        + [whole] * 5
        + [away] * 3
        + [whole] * 2
        + [away] * 2
        + [whole] * 5,
        out_specs=(whole, away, away, away, away),
        scratch_shapes=[
            pltpu.VMEM(out_full.shape, bf16),
            pltpu.VMEM(query_full.shape, bf16),
            pltpu.VMEM(pair_full.shape, bf16),
            pltpu.VMEM(key_all.shape, bf16),
            pltpu.VMEM(value_all.shape, bf16),
            pltpu.VMEM((rows, width), f32),
            pltpu.VMEM((rows, width), bf16),
            pltpu.VMEM((HEADS * rows, total_keys), bf16),
            pltpu.VMEM((HEADS * rows, total_keys), bf16),
            pltpu.VMEM((HEADS * rows, HEAD), bf16),
            pltpu.VMEM((HEADS * rows, HEAD), bf16),
            pltpu.VMEM((size, rows, 2 * HEAD), bf16),
            pltpu.VMEM((rows, qwidth), bf16),
            pltpu.VMEM(query_cols, bf16),
            pltpu.VMEM(pair_cols, bf16),
            pltpu.VMEM(proj_cols, bf16),
            pltpu.VMEM((8, width), f32),
            dma((9,)),
            dma((4, size - 1)),
            dma((4, size - 1)),
        ]
        + scatter_scratch(size, rows, width)
        + scatter_scratch(size, rows, 2 * HEAD),
        compiler_params=pltpu.CompilerParams(collective_id=ident, has_side_effects=True),
        cost_estimate=pl.CostEstimate(
            flops=0, bytes_accessed=30 * part.size * 2, transcendentals=0
        ),
        name=f"attn_back_{ident}",
    )(
        part,
        residual,
        cotangent,
        projected,
        tokens,
        gains,
        out_full,
        query_full,
        pair_full,
        attn_out,
        query_rot,
        key_all,
        value_all,
        queries,
        keys,
        cosine,
        sine,
        post_grad,
    )


def attn_front_kernel(
    dp,
    ctx,
    tokens,
    query_in,
    pair_in,
    out_in,
    gains_in,
    cosine,
    sine,
    residual,
    projected,
    queries,
    keys,
    query_rot,
    attn_out,
    key_all,
    value_all,
    gains,
    normed_hbm,
    query_hbm,
    pair_hbm,
    out_hbm,
    rows_all,
    attn_all,
    tokens_all,
    normed_all,
    query_w,
    pair_w,
    out_w,
    keys_all,
    gains_all,
    normed_two,
    local,
    far_send,
    far_recv,
    near_send,
    near_recv,
    pass_send,
    pass_recv,
    *scratch,
):
    rows, width = tokens.shape
    total_keys = key_all.shape[0]
    bf16, f32 = jnp.bfloat16, jnp.float32
    scaling = 1.0 / math.sqrt(HEAD)
    place = Place("ctx", ctx)
    me, row = place.me, lax.axis_index("dp")
    shard = query_in.shape[0]
    query_width = query_w.shape[1] // ctx
    pair_depth, pair_width = pair_in.shape
    out_shard = out_in.shape[0]
    out_depth = out_shard // ctx

    def query_region(source, base, origin):
        return source.at[
            pl.ds(pl.multiple_of(base * shard, 16), shard),
            pl.ds(pl.multiple_of(origin * query_width, 128), query_width),
        ]

    def pair_region(base, origin):
        start = base * shard + lax.rem(origin, 2) * pair_depth
        return pair_w.at[
            pl.ds(pl.multiple_of(start, 16), pair_depth),
            pl.ds(pl.multiple_of((origin // 2) * pair_width, 128), pair_width),
        ]

    def out_region(source, base, origin):
        start = base * out_shard + origin * out_depth
        return source.at[pl.ds(pl.multiple_of(start, 16), out_depth)]

    regions = (
        pair_region,
        functools.partial(query_region, query_w),
        functools.partial(out_region, out_w),
    )
    sources = (pair_in, query_region(query_in, 0, me), out_region(out_in, 0, me))
    pending = []

    def stay(source, target, index):
        copy = pltpu.make_async_copy(source, target, local.at[index])
        copy.start()
        return copy

    own = [stay(sources[item], regions[item](row, me), item) for item in range(3)]
    own.append(stay(gains_in, gains_all.at[row], 3))
    barrier = pltpu.get_barrier_semaphore()
    for step in range(1, place.half):
        pl.semaphore_signal(
            barrier, inc=1, device_id={"ctx": place.across(step)}, device_id_type=MESH
        )
    pl.semaphore_signal(barrier, inc=1, device_id={"ctx": place.twin}, device_id_type=MESH)
    for step in range(1, dp):
        pl.semaphore_signal(
            barrier, inc=1, device_id={"dp": lax.rem(row + step, dp)}, device_id_type=MESH
        )
    pl.semaphore_wait(barrier, place.half + dp - 1)

    far, near = {}, {}
    for item in (3, 0, 1, 2):
        for step in range(1, dp):
            far[item, step] = remote(
                gains_in if item == 3 else sources[item],
                gains_all.at[row] if item == 3 else regions[item](row, me),
                far_send.at[item, step - 1],
                far_recv.at[item, step - 1],
                "dp",
                lax.rem(row + step, dp),
            )
    token_gather = Gather(place, tokens, tokens_all, scratch[:5])
    row_gather = Gather(place, normed_two, rows_all, scratch[5:10])
    attn_gather = Gather(place, attn_out, attn_all, scratch[10:15])
    for index in range(len(token_gather.spans)):
        token_gather.start(index)

    def spread(item, lag):
        base = lax.rem(row + dp - lag, dp)
        if lag:
            far[item, lag].wait_recv()
        source = regions[item](base, me) if lag else sources[item]
        target = regions[item](base, me)
        for step in range(1, place.half):
            near[item, lag, step] = remote(
                source,
                target,
                near_send.at[item, lag, step],
                near_recv.at[item, lag, step],
                "ctx",
                place.across(step),
            )
        pending.append(
            remote(
                source,
                target,
                pass_send.at[item, lag, 0],
                pass_recv.at[item, lag, 0],
                "ctx",
                place.twin,
            )
        )
        item_passes[item].append(pending[-1])

    def relay(item):
        for lag in range(dp):
            base = lax.rem(row + dp - lag, dp)
            for step in range(1, place.half):
                near[item, lag, step].wait_recv()
                block = regions[item](base, place.behind(step))
                pending.append(
                    remote(
                        block,
                        block,
                        pass_send.at[item, lag, step],
                        pass_recv.at[item, lag, step],
                        "ctx",
                        place.twin,
                    )
                )
                item_passes[item].append(pending[-1])

    def complete(item):
        for copy in item_passes[item]:
            copy.wait_recv()
        own[item].wait()

    item_passes = ([], [], [])
    for item in range(3):
        spread(item, 0)
    token_gather.relay()
    for lag in range(1, dp):
        spread(0, lag)
    for step in range(1, dp):
        far[3, step].wait_recv()
    own[3].wait()
    total = gains_all[0]
    for step in range(1, dp):
        total = total + gains_all[step]
    gains[...] = total
    token_gather.finish()

    def normalize(block, carry):
        value = tokens_all[block].astype(f32)
        normed_all[block] = (value * inverse_rms(value) * gains[0:1]).astype(bf16)
        return carry

    lax.fori_loop(0, ctx, normalize, 0)
    saves = [stay(normed_all, normed_hbm, 4)]
    for lag in range(1, dp):
        spread(1, lag)
    relay(0)
    for lag in range(1, dp):
        spread(2, lag)
    complete(0)
    saves.append(stay(pair_w, pair_hbm, 5))

    def project(block, carry):
        both = matmul(normed_all[block], pair_w[...])
        value = both[:, :HEAD]
        turn = pl.ds(pl.multiple_of(block * rows, rows), rows)
        keys_all[block] = value
        key_all[turn] = rotate(
            value * inverse_rms(value) * gains[4:5, HEAD : 2 * HEAD], cosine[turn], sine[turn]
        ).astype(bf16)
        value_all[turn] = both[:, HEAD:].astype(bf16)
        return carry

    lax.fori_loop(0, ctx, project, 0)
    keys[...] = keys_all[me]
    relay(1)
    complete(1)
    saves.append(stay(query_w, query_hbm, 6))
    queries[...] = matmul(normed_all[me], query_w[...])
    here = pl.ds(pl.multiple_of(me * rows, rows), rows)

    def attend(head, carry):
        lanes = pl.ds(pl.multiple_of(head * HEAD, HEAD), HEAD)
        query_pos = me * rows + lax.broadcasted_iota(jnp.int32, (rows, total_keys), 0)
        allowed = query_pos >= lax.broadcasted_iota(jnp.int32, (rows, total_keys), 1)
        value = queries[:, lanes]
        query = (
            rotate(value * inverse_rms(value) * gains[4:5, :HEAD], cosine[here], sine[here])
            * scaling
        ).astype(bf16)
        query_rot[:, lanes] = query
        scores = jnp.where(allowed, matmul_nt(query, key_all[...]), NEG_FILL)
        weights = jnp.where(
            allowed, jnp.exp(scores - jnp.max(scores, axis=-1, keepdims=True)), 0.0
        )
        attn_out[:, lanes] = (
            matmul(weights.astype(bf16), value_all[...]) / jnp.sum(weights, axis=-1, keepdims=True)
        ).astype(bf16)
        return carry

    lax.fori_loop(0, HEADS, attend, 0)
    relay(2)
    complete(2)
    saves.append(stay(out_w, out_hbm, 7))
    projected[...] = matmul(attn_out[...], out_w[...])
    for index, span in enumerate(row_gather.spans):
        ahead = projected[span]
        kept = tokens[span].astype(f32) + ahead * inverse_rms(ahead) * gains[1:2]
        residual[span] = kept
        normed_two[span] = (kept * inverse_rms(kept) * gains[2:3]).astype(bf16)
        row_gather.start(index)
    for index in range(len(attn_gather.spans)):
        attn_gather.start(index)
    row_gather.relay()
    attn_gather.relay()
    row_gather.finish()
    attn_gather.finish()
    for copy in list(far.values()) + list(near.values()) + pending:
        copy.wait_send()
    for copy in saves:
        copy.wait()


def attn_front(tokens, query_weight, pair, out_weight, gain_rows, cosine, sine, dp, ctx, ident):
    rows, width = tokens.shape
    shard, qwidth = query_weight.shape
    half = ctx // 2
    pair_depth, pair_width = shard // 2, pair.shape[1] // half
    index = lax.axis_index("ctx")
    pair_slice = lax.dynamic_slice(
        pair, (lax.rem(index, 2) * pair_depth, index // 2 * pair_width), (pair_depth, pair_width)
    )
    bf16, f32 = jnp.bfloat16, jnp.float32
    whole = pl.BlockSpec(memory_space=pltpu.VMEM)
    away = pl.BlockSpec(memory_space=pl.ANY)
    dma = pltpu.SemaphoreType.DMA
    vmem, shape = pltpu.VMEM, jax.ShapeDtypeStruct
    query_full, pair_full = (dp * shard, qwidth), (dp * shard, pair.shape[1])
    out_full = (dp * out_weight.shape[0], width)
    return pl.pallas_call(
        functools.partial(attn_front_kernel, dp, ctx),
        out_shape=(
            shape((rows, width), f32),
            shape((rows, width), f32),
            shape((rows, qwidth), f32),
            shape((rows, HEAD), f32),
            shape((rows, qwidth), bf16),
            shape((rows, qwidth), bf16),
            shape((ctx * rows, HEAD), bf16),
            shape((ctx * rows, HEAD), bf16),
            shape((8, width), f32),
            shape((ctx, rows, width), bf16),
            shape(query_full, bf16),
            shape(pair_full, bf16),
            shape(out_full, bf16),
            shape((ctx, rows, width), bf16),
            shape((ctx, rows, qwidth), bf16),
        ),
        in_specs=[whole, away, whole, away, whole, whole, whole],
        out_specs=(whole,) * 9 + (away,) * 6,
        scratch_shapes=[
            vmem((ctx, rows, width), bf16),
            vmem((ctx, rows, width), bf16),
            vmem(query_full, bf16),
            vmem(pair_full, bf16),
            vmem(out_full, bf16),
            vmem((ctx, rows, HEAD), f32),
            vmem((dp, 8, width), f32),
            vmem((rows, width), bf16),
            dma((8,)),
            dma((4, dp - 1)),
            dma((4, dp - 1)),
        ]
        + [dma((3, dp, half))] * 4
        + gather_scratch(ctx, rows) * 3,
        compiler_params=pltpu.CompilerParams(collective_id=ident, has_side_effects=True),
        cost_estimate=pl.CostEstimate(
            flops=0, bytes_accessed=100 * ctx * rows * width, transcendentals=0
        ),
        name=f"attn_front_{ident}",
    )(tokens, query_weight, pair_slice, out_weight, gain_rows, cosine, sine)


def fits_front(shard, qwidth, pair_width, out_shard, ctx):
    return (
        ctx % 2 == 0
        and qwidth % (128 * ctx) == 0
        and pair_width % (64 * ctx) == 0
        and shard % 32 == 0
        and out_shard % (16 * ctx) == 0
    )


def gain_block(gains, width):
    gain_in, gain_query, gain_key, gain_attn, gain_pre, gain_post = gains
    heads = jnp.concatenate([gain_query, gain_key])
    heads = jnp.pad(heads, (0, width - heads.shape[0]))
    stacked = jnp.stack([gain_in, gain_attn, gain_pre, gain_post, heads])
    return jnp.pad(stacked, ((0, 3), (0, 0)))


def spread_gain(gain, dp):
    place = jnp.arange(dp * gain.shape[0], dtype=jnp.int32) // gain.shape[0]
    tiled = jnp.tile(gain.astype(jnp.float32), dp)
    return jnp.where(place == lax.axis_index("dp"), tiled, 0.0)


def by_rows(array):
    return with_layout_constraint(array, Layout(major_to_minor=(0, 1)))


def by_columns(array, parts):
    rows, columns = array.shape
    return jnp.transpose(array.reshape(rows, parts, columns // parts), (1, 0, 2))


def from_columns(array):
    parts, rows, columns = array.shape
    return jnp.transpose(array, (1, 0, 2)).reshape(rows, parts * columns)


def sum_blocks(array):
    return jnp.sum(array.astype(jnp.float32), axis=0)


def plain_front(
    tokens, query_weight, pair, out_weight, raw_gains, cuts, cosine_all, sine_all, dp, ctx
):
    rows, width = tokens.shape
    bf16 = jnp.bfloat16
    scaling = 1.0 / math.sqrt(HEAD)
    ctx_index = lax.axis_index("ctx")
    query_pos = ctx_index * rows + jnp.arange(rows, dtype=jnp.int32)
    cosine = lax.dynamic_slice_in_dim(cosine_all, ctx_index * rows, rows, 0)
    sine = lax.dynamic_slice_in_dim(sine_all, ctx_index * rows, rows, 0)
    kwidth = pair.shape[1] // 2
    query_columns = query_weight.shape[1] // ctx
    pair_rows = pair.shape[0] // ctx
    out_rows = out_weight.shape[0] // ctx
    query_slice = lax.dynamic_slice_in_dim(query_weight, ctx_index * query_columns, query_columns, 1)
    pair_slice = lax.dynamic_slice_in_dim(pair, ctx_index * pair_rows, pair_rows, 0)
    out_slice = lax.dynamic_slice_in_dim(out_weight, ctx_index * out_rows, out_rows, 0)
    packed_gains = jnp.concatenate([gain.astype(jnp.float32) for gain in raw_gains])[None]
    query_dp, pair_dp, out_dp, gains_dp = exchange(
        (query_slice, pair_slice, out_slice, packed_gains), ("gather",) * 4, "dp", dp, 0
    )
    gains_dp = gains_dp[:, 0]
    gain_in, gain_query, gain_key, gain_attn, gain_pre, gain_post = (
        gains_dp[:, low:high].reshape(-1) for low, high in zip(cuts[:-1], cuts[1:])
    )
    query_all, pair_all, out_all, tokens_all = exchange(
        (query_dp.reshape(-1, query_columns), pair_dp, out_dp, tokens),
        ("gather",) * 4,
        "ctx",
        ctx,
        1,
    )
    query_full = from_columns(query_all)
    pair_full = jnp.transpose(pair_all, (1, 0, 2, 3)).reshape(-1, 2 * kwidth)
    key_full = pair_full[:, :kwidth]
    value_full = pair_full[:, kwidth:]
    out_full = jnp.transpose(out_all, (1, 0, 2, 3)).reshape(-1, out_weight.shape[1])

    inputs_f = tokens.astype(jnp.float32)
    inv_one = inverse_rms(inputs_f)
    normed_one = (inputs_f * inv_one * gain_in).astype(bf16)
    all_f = tokens_all.reshape(-1, width).astype(jnp.float32)
    normed_all = (all_f * inverse_rms(all_f) * gain_in).astype(bf16)
    key_pos = jnp.arange(all_f.shape[0], dtype=jnp.int32)
    queries = matmul(normed_one, query_full).reshape(rows, HEADS, HEAD)
    keys = matmul(normed_one, key_full)
    keys_every = matmul(normed_all, key_full)
    value_all = matmul(normed_all, value_full).astype(bf16)
    inv_query = inverse_rms(queries)
    inv_key = inverse_rms(keys)
    query_rot = (
        rotate(queries * inv_query * gain_query, cosine[:, None, :], sine[:, None, :]) * scaling
    ).astype(bf16)
    key_all = rotate(
        keys_every * inverse_rms(keys_every) * gain_key, cosine_all, sine_all
    ).astype(bf16)
    allowed = (query_pos[:, None] >= key_pos[None, :])[None]
    scores = jnp.einsum("qhd,kd->hqk", query_rot, key_all, preferred_element_type=jnp.float32)
    scores = jnp.where(allowed, scores, NEG_FILL)
    row_max = jnp.max(scores, axis=-1, keepdims=True)
    weights = jnp.where(allowed, jnp.exp(scores - row_max), 0.0)
    total = jnp.sum(weights, axis=-1, keepdims=True)
    accum = jnp.einsum(
        "hqk,kd->hqd", weights.astype(bf16), value_all, preferred_element_type=jnp.float32
    )
    attn_heads = jnp.transpose(accum / total, (1, 0, 2)).astype(bf16)
    attn_out = attn_heads.reshape(rows, HEADS * HEAD)
    projected = matmul(attn_out, out_full)
    inv_proj = inverse_rms(projected)
    residual = inputs_f + projected * inv_proj * gain_attn
    inv_two = inverse_rms(residual)
    normed_two = (residual * inv_two * gain_pre).astype(bf16)

    rows_all, attn_all = exchange((normed_two, attn_out), ("gather",) * 2, "ctx", ctx, 2)
    gains = gain_block(
        [gain_in, gain_query, gain_key, gain_attn, gain_pre, gains_dp[:, cuts[-2] :].reshape(-1)], width
    )
    return (
        residual,
        projected,
        queries.reshape(rows, HEADS * HEAD),
        keys,
        query_rot.reshape(rows, HEADS * HEAD),
        attn_out,
        key_all,
        value_all,
        gains,
        normed_all,
        query_full,
        pair_full,
        out_full,
        rows_all,
        attn_all,
    )


def on_device(
    dp,
    ctx,
    tokens,
    in_gain,
    query_weight,
    key_weight,
    value_weight,
    query_gain,
    key_gain,
    out_weight,
    attn_post_gain,
    ffn_pre_gain,
    gate_weight,
    up_weight,
    down_weight,
    ffn_post_gain,
    cotangent,
):
    rows, width = tokens.shape
    bf16 = jnp.bfloat16
    qwidth = query_weight.shape[1]
    kwidth = key_weight.shape[1]
    out_columns = out_weight.shape[1] // ctx
    query_columns = qwidth // ctx
    pair = jnp.concatenate([key_weight, value_weight], axis=1)
    raw_gains = (in_gain, query_gain, key_gain, attn_post_gain, ffn_pre_gain, ffn_post_gain)
    cuts = [0]
    for gain in raw_gains:
        cuts.append(cuts[-1] + gain.shape[0])
    key_pos = jnp.arange(ctx * rows, dtype=jnp.int32)
    cosine_all, sine_all = rope_tables(key_pos.astype(jnp.float32))
    gate_full, up_full, down_full = (
        lax.all_gather(gate_weight, "dp", axis=0, tiled=True),
        lax.all_gather(up_weight, "dp", axis=0, tiled=True),
        lax.all_gather(down_weight, "dp", axis=0, tiled=True),
    )
    if fits_front(query_weight.shape[0], qwidth, 2 * kwidth, out_weight.shape[0], ctx):
        gain_rows = gain_block([spread_gain(gain, dp) for gain in raw_gains], width)
        (
            residual,
            projected,
            queries,
            keys,
            query_rot,
            attn_out,
            key_all,
            value_all,
            gains,
            normed_all,
            query_full,
            pair_full,
            out_full,
            rows_all,
            attn_all,
        ) = attn_front(
            tokens, query_weight, pair, out_weight, gain_rows, cosine_all, sine_all, dp, ctx, 10
        )
    else:
        (
            residual,
            projected,
            queries,
            keys,
            query_rot,
            attn_out,
            key_all,
            value_all,
            gains,
            normed_all,
            query_full,
            pair_full,
            out_full,
            rows_all,
            attn_all,
        ) = plain_front(
            tokens, query_weight, pair, out_weight, raw_gains, cuts, cosine_all, sine_all, dp, ctx
        )
    normed_all = normed_all.reshape(-1, width)
    attn_all = attn_all.reshape(-1, qwidth)
    rows_all = rows_all.reshape(-1, width)
    gate = matmul(rows_all, gate_full)
    upper = matmul(rows_all, up_full)
    gelu_val, gelu_der = gelu_pair(gate)
    hidden = (gelu_val * upper).astype(bf16)
    ffn_part = matmul_nt(hidden, down_full).astype(bf16).reshape(ctx, rows, width)
    block_out, grad_post, grad_all = ffn_turn(
        ffn_part, residual, cotangent, gains[3:4], "ctx", ctx, 3
    )
    grad_all = grad_all.reshape(-1, width)
    down_part, grad_all = lax.optimization_barrier(
        (by_rows(matmul_tn(grad_all, hidden).astype(bf16)), grad_all)
    )
    down_shard = lax.psum_scatter(down_part, "dp", scatter_dimension=0, tiled=True)
    down_shard = down_shard.astype(jnp.float32)
    hidden_grad = matmul(grad_all, down_full)
    gate_grad = (hidden_grad * upper * gelu_der).astype(bf16)
    up_grad = (hidden_grad * gelu_val).astype(bf16)
    gate_part = by_rows(matmul_tn(rows_all, gate_grad).astype(bf16))
    up_part = by_rows(matmul_tn(rows_all, up_grad).astype(bf16))
    gate_shard = lax.psum_scatter(gate_part, "dp", scatter_dimension=0, tiled=True)
    gate_shard = gate_shard.astype(jnp.float32)
    two_part = (matmul_nt(gate_grad, gate_full) + matmul_nt(up_grad, up_full)).astype(bf16)
    input_grad, query_cols, pair_cols, proj_cols, all_gains = attn_back(
        two_part.reshape(ctx, rows, width),
        residual,
        cotangent,
        projected,
        tokens,
        gains,
        out_full,
        query_full,
        pair_full,
        attn_out,
        query_rot,
        key_all,
        value_all,
        queries,
        keys,
        cosine_all,
        sine_all,
        grad_post,
        "ctx",
        ctx,
        5,
    )
    gain_sums = jnp.sum(all_gains, axis=0)
    gain_grads = (
        gain_sums[0],
        gain_sums[4, :HEAD],
        gain_sums[5, :HEAD],
        gain_sums[1],
        gain_sums[2],
        gain_sums[3],
    )
    packed = jnp.concatenate([grad.reshape(dp, -1) for grad in gain_grads], axis=1)
    query_w = matmul_tn(normed_all, query_cols.reshape(-1, query_columns)).astype(bf16)
    pair_w = matmul_tn(normed_all, pair_cols.reshape(normed_all.shape[0], -1)).astype(bf16)
    out_w = matmul_tn(attn_all, proj_cols.reshape(-1, out_columns)).astype(bf16)
    query_w, pair_w, out_w, gain_parts = exchange(
        (
            query_w.reshape(dp, -1, query_columns),
            pair_w.reshape(dp, -1, pair_w.shape[1]),
            out_w.reshape(dp, -1, out_columns),
            packed[:, None],
        ),
        ("swap",) * 4,
        "dp",
        dp,
        8,
    )
    up_part, query_w, pair_w, out_w = lax.optimization_barrier((up_part, query_w, pair_w, out_w))
    up_shard = lax.psum_scatter(up_part, "dp", scatter_dimension=0, tiled=True)
    up_shard = up_shard.astype(jnp.float32)
    query_w, pair_w, out_w = exchange(
        (sum_blocks(query_w).astype(bf16), sum_blocks(pair_w).astype(bf16), sum_blocks(out_w).astype(bf16)),
        ("gather",) * 3,
        "ctx",
        ctx,
        9,
    )
    query_w = from_columns(query_w).astype(jnp.float32)
    pair_w = from_columns(pair_w).astype(jnp.float32)
    out_w = from_columns(out_w).astype(jnp.float32)
    gain_done = sum_blocks(gain_parts).reshape(-1)
    share = [gain_done[low:high] for low, high in zip(cuts[:-1], cuts[1:])]
    return (
        block_out,
        input_grad,
        share[0],
        query_w,
        pair_w[:, :kwidth],
        pair_w[:, kwidth:],
        share[1],
        share[2],
        out_w,
        share[3],
        share[4],
        gate_shard,
        up_shard,
        down_shard,
        share[5],
    )


def solution(mesh):
    return jax.shard_map(
        functools.partial(on_device, mesh.shape["dp"], mesh.shape["ctx"]),
        mesh=mesh,
        in_specs=(
            P(("dp", "ctx"), None),
            P("dp"),
            P("dp", None),
            P("dp", None),
            P("dp", None),
            P("dp"),
            P("dp"),
            P("dp", None),
            P("dp"),
            P("dp"),
            P("dp", "ctx"),
            P("dp", "ctx"),
            P("dp", "ctx"),
            P("dp"),
            P(("dp", "ctx"), None),
        ),
        out_specs=(
            P(("dp", "ctx"), None),
            P(("dp", "ctx"), None),
            P("dp"),
            P("dp", None),
            P("dp", None),
            P("dp", None),
            P("dp"),
            P("dp"),
            P("dp", None),
            P("dp"),
            P("dp"),
            P("dp", "ctx"),
            P("dp", "ctx"),
            P("dp", "ctx"),
            P("dp"),
        ),
        check_vma=False,
    )
```

profile of v0, /device:TPU:0, one launch (start us, length us, event | category | flops | bytes accessed | tf_op | source)
XLA Modules:
  0.0 384.7 jit_solution(9014197728620200242)
XLA Ops:
  16.2 3.0 multiply_sine_fusion
  19.2 90.8 %attn_front_10.1 = (f32[128,1152]{1,0:T(8,128)}, f32[128,1152]{1,0:T(8,128)}, f32[128,1024]{1,0:T(8,128)}, f32[128,256]{1,0:T(8,128)}, bf16[128,1024]{1,0:T(8,12...) custom-call(bf16[128,1152]{1,0:T(8,128)(2,1)} %tokens.3, ...), custom_call_target="tpu_custom_call" | custom-call | bytes 117964800 | tf_op jit(solution)/shard_map/attn_front_10/pallas_call | solution.py:1048
  111.5 6.7 %fusion.14 = f32[1024,864]{0,1:T(8,128)} fusion(bf16[1024,1152]{1,0:T(8,128)(2,1)} %bitcast.66, bf16[1152,864]{1,0:T(8,128)(2,1)} %all-gather.4.cloned.1.call-done), kind=kOutput, calls=%fused_computation.65 | convolution fusion | flops 2038431744 | bytes 7888896 | tf_op jit(solution)/shard_map/dot_general | solution.py:69
  118.2 3.7 all-gather.6.cloned.1.call-done
  121.8 8.3 %multiply_convert_fusion.1 = (bf16[1024,864]{0,1:T(8,128)(2,1)}, f32[1024,864]{0,1:T(8,128)}) fusion(f32[1024,864]{0,1:T(8,128)} %fusion.14, bf16[1024,1152]{1,0:T(8,128)(2,1)S(1)} %bitcast.68, bf16[1152,864]{1,0:T(8,128)(2,1)} %all-gather.6.cloned.1.call-done), kind=kOutput, calls=%fused_computation.15 | convolution fusion | flops 2047279104 | bytes 13197312 | tf_op jit(solution)/shard_map/dot_general | solution.py:69
  130.1 37.2 %all-gather.8.cloned.1.call-done = bf16[1152,864]{1,0:T(8,128)(2,1)} async-done(((bf16[288,864]{1,0:T(8,128)(2,1)}), bf16[1152,864]{1,0:T(8,128)(2,1)}) %all-gather.8.cloned.1.call-update) | async-done | bytes 1990672 | tf_op jit(solution)/shard_map/all_gather | solution.py:1265
  167.4 6.4 %convolution_convert_fusion = bf16[1024,1152]{1,0:T(8,128)(2,1)} fusion(bf16[1024,864]{0,1:T(8,128)(2,1)} %get-tuple-element.120, bf16[1152,864]{1,0:T(8,128)(2,1)} %all-gather.8.cloned.1.call-done), kind=kOutput, calls=%fused_computation.3 | convolution fusion | flops 2039611392 | bytes 6119424 | tf_op jit(solution)/shard_map/dot_general | solution.py:79
  173.8 34.6 %ffn_turn_3.1 = (bf16[128,1152]{1,0:T(8,128)(2,1)}, f32[1,1152]{1,0:T(1,128)}, bf16[8,128,1152]{2,1,0:T(8,128)(2,1)}) custom-call(bf16[8,128,1152]{2,1,0:T(8,128)(2,1)} %bitcast.61, f32[128,1152]{1,0:T(8,128)} %get-tuple-element.52.residual, bf16[128,1152]{1,0:T(8,128)(2,1)} %cot.3, f32[1,1152]{1,0:T(1,128)} %slice.63.gain), custom_call_target="tpu_custom_call" | custom-call | bytes 47185920 | tf_op jit(solution)/shard_map/ffn_turn_3/pallas_call | solution.py:445
  208.4 6.1 %convolution_convert_fusion.3 = bf16[1152,864]{1,0:T(8,128)(2,1)} fusion(bf16[1024,1152]{1,0:T(8,128)(2,1)} %bitcast.70, bf16[1024,864]{0,1:T(8,128)(2,1)} %get-tuple-element.120), kind=kOutput, calls=%fused_computation.6 | convolution fusion | flops 2039427072 | bytes 6119424 | tf_op jit(solution)/shard_map/dot_general | solution.py:73
  214.6 10.4 %multiply_convert_fusion = (bf16[1024,864]{0,1:T(8,128)(2,1)}, bf16[1024,864]{0,1:T(8,128)(2,1)S(1)}) fusion(f32[1024,864]{0,1:T(8,128)} %fusion.14, f32[1024,864]{0,1:T(8,128)} %get-tuple-element.121, bf16[1024,1152]{1,0:T(8,128)(2,1)} %bitcast.71, bf16[1152,864]{1,0:T(8,128)(2,1)} %all-gather.8.cloned.1.call-done), kind=kOutput, calls=%fused_computation.14 | convolution fusion | flops 2058780672 | bytes 14966784 | tf_op jit(solution)/shard_map/dot_general | solution.py:69
  226.2 4.0 %convolution_convert_fusion.1 = bf16[1152,864]{1,0:T(8,128)(2,1)} fusion(bf16[1024,1152]{1,0:T(8,128)(2,1)S(1)} %bitcast.69, bf16[1024,864]{0,1:T(8,128)(2,1)S(1)} %get-tuple-element.113), kind=kOutput, calls=%fused_computation.4 | convolution fusion | flops 2039427072 | bytes 6119424 | tf_op jit(solution)/shard_map/dot_general | solution.py:73
  230.6 5.2 %fusion.15 = f32[1024,1152]{1,0:T(8,128)S(1)} fusion(bf16[1024,864]{0,1:T(8,128)(2,1)} %copy-done.13, bf16[1152,864]{1,0:T(8,128)(2,1)} %all-gather.4.cloned.1.call-done), kind=kOutput, calls=%fused_computation.66 | convolution fusion | flops 2038431744 | bytes 8478720 | tf_op jit(solution)/shard_map/dot_general | solution.py:79
  235.8 4.3 %add_convert_fusion = bf16[1024,1152]{1,0:T(8,128)(2,1)} fusion(f32[1024,1152]{1,0:T(8,128)S(1)} %fusion.15, bf16[1024,864]{0,1:T(8,128)(2,1)S(1)} %copy-done.14, bf16[1152,864]{1,0:T(8,128)(2,1)S(1)} %copy-done.11), kind=kOutput, calls=%fused_computation.2 | convolution fusion | flops 2040791040 | bytes 10838016 | tf_op jit(solution)/shard_map/dot_general | solution.py:79
  240.1 46.2 %attn_back_5.1 = (f32[128,1152]{1,0:T(8,128)}, bf16[8,128,128]{2,1,0:T(8,128)(2,1)}, bf16[8,128,64]{2,1,0:T(8,128)(2,1)}, bf16[8,128,144]{2,1,0:T(8,128)(2,1)}, f32[8,8,1152]{2,1,0:T(8,128)}) custom-call(bf16[8,128,1152]{2,1,0:T(8,128)(2,1)} %bitcast.62, f32[128,1152]{1,0:T(8,128)} %get-tuple-element.52.residual, bf16[128,1152]{1,0:T(8,128)(2,1)} %cot.3, ...), custom_call_target="tpu_custom_call" | custom-call | bytes 70778880 | tf_op jit(solution)/shard_map/attn_back_5/pallas_call | solution.py:709
  288.7 1.5 fusion.8
  291.0 2.2 fusion.9
  294.2 1.5 fusion.7
  295.7 29.5 %exchange_8.1 = (bf16[4,288,128]{2,1,0:T(8,128)(2,1)}, bf16[4,288,64]{2,1,0:T(8,128)(2,1)}, bf16[4,256,144]{2,1,0:T(8,128)(2,1)}, f32[4,1,1280]{2,1,0:T(1,128)}) custom-call(bf16[4,288,128]{2,1,0:T(8,128)(2,1)} %bitcast.64, bf16[4,288,64]{2,1,0:T(8,128)(2,1)} %bitcast.65, bf16[4,256,144]{2,1,0:T(8,128)(2,1)} %bitcast.63, f32[4,1,1280]{2,1,0:T(1,128)} %broadcast_in_dim.19.refs_3_), custom_call_target="tpu_custom_call" | custom-call | bytes 15155200 | tf_op jit(solution)/shard_map/exchange_8/pallas_call | solution.py:222
  325.3 6.2 %convolution_convert_fusion.2 = bf16[1152,864]{1,0:T(8,128)(2,1)} fusion(bf16[1024,1152]{1,0:T(8,128)(2,1)} %bitcast.67, bf16[1024,864]{0,1:T(8,128)(2,1)} %get-tuple-element.112), kind=kOutput, calls=%fused_computation.5 | convolution fusion | flops 2039427072 | bytes 6119424 | tf_op jit(solution)/shard_map/dot_general | solution.py:73
  334.0 18.9 %exchange_9.1 = (bf16[8,288,128]{2,1,0:T(8,128)(2,1)}, bf16[8,288,64]{2,1,0:T(8,128)(2,1)}, bf16[8,256,144]{2,1,0:T(8,128)(2,1)}) custom-call(bf16[288,128]{1,0:T(8,128)(2,1)} %reduce_sum.59.refs_0_, bf16[288,64]{1,0:T(8,128)(2,1)} %reduce_sum.60.refs_1_, bf16[256,144]{1,0:T(8,128)(2,1)} %reduce_sum.61.refs_2_), custom_call_target="tpu_custom_call" | custom-call | bytes 29491200 | tf_op jit(solution)/shard_map/exchange_9/pallas_call | solution.py:222
  361.1 2.1 convert_element_type.139
  363.2 2.1 convert_element_type.137
  365.3 8.7 %reduce-scatter.6.cloned.1.call-done = bf16[288,864]{1,0:T(8,128)(2,1)} async-done(((bf16[1152,864]{1,0:T(8,128)(2,1)}), bf16[288,864]{1,0:T(8,128)(2,1)}) %reduce-scatter.6.cloned.1.call-update) | async-done | bytes 497680 | tf_op jit(solution)/shard_map/reduce_scatter | solution.py:1382
  373.9 2.1 convert_element_type.138
  (99 shorter events, 28.1 us)
Async XLA Ops:
  7.2 104.3 %all-gather.4.cloned.1.call-start = ((), (), s32[]{:S(2)}) async-start(), calls=%async_computation.3 | async-start | bytes 2580480 | tf_op jit(solution)/shard_map/all_gather | solution.py:1263
  7.9 113.9 %all-gather.6.cloned.1.call-start = ((), (), s32[]{:S(2)}) async-start(), calls=%async_computation.4 | async-start | bytes 2580480 | tf_op jit(solution)/shard_map/all_gather | solution.py:1264
  8.7 158.7 %all-gather.8.cloned.1.call-start = ((), (), s32[]{:S(2)}) async-start(), calls=%async_computation.5 | async-start | bytes 2580480 | tf_op jit(solution)/shard_map/all_gather | solution.py:1265
  9.4 351.7 %reduce-scatter.8.cloned.1.call-start = ((), (), s32[]{:S(2)}) async-start(), calls=%async_computation.8 | async-start | bytes 2580480 | tf_op jit(solution)/shard_map/reduce_scatter | solution.py:1323
  111.5 10.4 %copy-start.10 = (bf16[8,128,1152]{2,1,0:T(8,128)(2,1)S(1)}, bf16[8,128,1152]{2,1,0:T(8,128)(2,1)}, u32[]{:S(2)}) copy-start(bf16[8,128,1152]{2,1,0:T(8,128)(2,1)} %get-tuple-element.51) | copy-start | bytes 7077892
  214.6 148.6 %reduce-scatter.4.cloned.1.call-start = ((), (), s32[]{:S(2)}) async-start(), calls=%async_computation.6 | async-start | bytes 2580480 | tf_op jit(solution)/shard_map/reduce_scatter | solution.py:1330
  225.1 1.2 copy-start.13
  230.3 5.5 %copy-start.11 = (bf16[1152,864]{1,0:T(8,128)(2,1)S(1)}, bf16[1152,864]{1,0:T(8,128)(2,1)}, u32[]{:S(2)}) copy-start(bf16[1152,864]{1,0:T(8,128)(2,1)} %all-gather.6.cloned.1.call-done) | copy-start | bytes 5971972
  230.3 143.7 %reduce-scatter.6.cloned.1.call-start = ((), (), s32[]{:S(2)}) async-start(), calls=%async_computation.7 | async-start | bytes 2580480 | tf_op jit(solution)/shard_map/reduce_scatter | solution.py:1382
  230.5 5.2 %copy-start.14 = (bf16[1024,864]{0,1:T(8,128)(2,1)S(1)}, bf16[1024,864]{0,1:T(8,128)(2,1)}, u32[]{:S(2)}) copy-start(bf16[1024,864]{0,1:T(8,128)(2,1)} %get-tuple-element.112) | copy-start | bytes 5308420
  240.1 48.6 %copy-start = (bf16[8,128,1152]{2,1,0:T(8,128)(2,1)S(1)}, bf16[8,128,1152]{2,1,0:T(8,128)(2,1)}, u32[]{:S(2)}) copy-start(bf16[8,128,1152]{2,1,0:T(8,128)(2,1)} %get-tuple-element.69) | copy-start | bytes 7077892
  287.8 3.2 copy-start.12
  291.0 3.2 copy-start.8
  325.3 6.3 %copy-start.9 = (f32[4,1,1280]{2,1,0:T(1,128)S(1)}, f32[4,1,1280]{2,1,0:T(1,128)}, u32[]{:S(2)}) copy-start(f32[4,1,1280]{2,1,0:T(1,128)} %get-tuple-element.75) | copy-start | bytes 61444
  325.3 6.3 %copy-start.7 = (bf16[4,288,128]{2,1,0:T(8,128)(2,1)S(1)}, bf16[4,288,128]{2,1,0:T(8,128)(2,1)}, u32[]{:S(2)}) copy-start(bf16[4,288,128]{2,1,0:T(8,128)(2,1)} %get-tuple-element.79) | copy-start | bytes 884740
  331.5 1.0 copy-start.6
  331.5 1.7 copy-start.4
  354.0 2.2 copy-start.1
  357.2 2.7 copy-start.2
  361.1 14.9 %copy-start.5 = (bf16[128,1152]{1,0:T(8,128)(2,1)S(1)}, bf16[128,1152]{1,0:T(8,128)(2,1)}, u32[]{:S(2)}) copy-start(bf16[128,1152]{1,0:T(8,128)(2,1)} %get-tuple-element.143) | copy-start | bytes 884740
  361.1 15.7 %copy-start.3 = (f32[128,1152]{1,0:T(8,128)S(1)}, f32[128,1152]{1,0:T(8,128)}, u32[]{:S(2)}) copy-start(f32[128,1152]{1,0:T(8,128)} %get-tuple-element.144) | copy-start | bytes 1769476
Sparse Core Ops, SparseCore 0:
  9.6 66.8 all-gather.3
  78.0 43.7 all-gather.5
  123.4 43.9 all-gather.7
  214.7 42.4 reduce-scatter.7
  259.3 42.2 reduce-scatter.3
  331.7 42.2 reduce-scatter.5
where the time goes:
time: 388 us; the launch traced here: 385 us
  Pallas kernels  220 us (57%)
  matrix products  62.9 us (16%)
  waiting for transfers between devices  51.6 us (13%)
  local copies, waits for them, and re-layouts  18.4 us (5%)
  other arithmetic  16.4 us (4%)
  between operations  14.7 us (4%)
    pallas_call x1, Pallas kernels, attn_front(): pl.pallas_call(functools.partial(attn_front_kernel, dp, ctx), out_shape=(...  90.8 us
    pallas_call x2, Pallas kernels, exchange(): pl.pallas_call(functools.partial(body, size, axis, tuple(kinds)), out_sha...  48.4 us
    pallas_call x1, Pallas kernels, attn_back(): pl.pallas_call(functools.partial(attn_back_kernel, axis, size), out_shape...  46.2 us
    all_gather x1, waiting for transfers between devices, on_device(): lax.all_gather(down_weight, 'dp', axis=0, tiled=True)  37.2 us
    pallas_call x1, Pallas kernels, ffn_turn(): pl.pallas_call(functools.partial(ffn_turn_kernel, axis, size), out_shape=...  34.6 us
    dot_general x3, matrix products, matmul(): return jnp.dot(left, right, preferred_element_type=jnp.float32)  25.5 us
    dot_general x6, matrix products, matmul_tn(): lax.dot_general(left, right, (((0,), (0,)), ((), ())), preferred_element_...  21.5 us
    dot_general x3, matrix products, matmul_nt(): lax.dot_general(left, right, (((1,), (1,)), ((), ())), preferred_element_...  15.9 us
  transfers between devices with their start and end apart: 6, of which 3 were waited for; matrix products, arithmetic and copies ran while one was open for 21% of the time, Pallas kernels for 48%

commit v1 on v0

--- a/solution.py
+++ b/solution.py
@@ -1330,6 +1330,7 @@
     gate_shard = lax.psum_scatter(gate_part, "dp", scatter_dimension=0, tiled=True)
     gate_shard = gate_shard.astype(jnp.float32)
     two_part = (matmul_nt(gate_grad, gate_full) + matmul_nt(up_grad, up_full)).astype(bf16)
+    two_part, up_part = lax.optimization_barrier((two_part, up_part))
     input_grad, query_cols, pair_cols, proj_cols, all_gains = attn_back(
         two_part.reshape(ctx, rows, width),
         residual,

time: 388 us -> 391 us (level)
    dot_general x3, matrix products: 15.9 us -> 21.6 us  [matmul_nt(): lax.dot_general(left, right, (((1,), (1,)), ((), ())), preferred_element_...]
  transfers between devices with their start and end apart: 6 -> 6, of which waited for: 3 -> 3; matrix products, arithmetic and copies ran while one was open for 21% -> 22% of each run, Pallas kernels for 48% -> 48%
where the time goes in v1:
time: 391 us; the launch traced here: 388 us
  Pallas kernels  219 us (56%)
  matrix products  66.5 us (17%)
  waiting for transfers between devices  50.2 us (13%)
  local copies, waits for them, and re-layouts  18.3 us (5%)
  other arithmetic  18.2 us (5%)
  between operations  14.6 us (4%)
    pallas_call x1, Pallas kernels, attn_front(): pl.pallas_call(functools.partial(attn_front_kernel, dp, ctx), out_shape=(...  90.8 us
    pallas_call x2, Pallas kernels, exchange(): pl.pallas_call(functools.partial(body, size, axis, tuple(kinds)), out_sha...  47.1 us
    pallas_call x1, Pallas kernels, attn_back(): pl.pallas_call(functools.partial(attn_back_kernel, axis, size), out_shape...  46.9 us
    all_gather x1, waiting for transfers between devices, on_device(): lax.all_gather(down_weight, 'dp', axis=0, tiled=True)  37.2 us
    pallas_call x1, Pallas kernels, ffn_turn(): pl.pallas_call(functools.partial(ffn_turn_kernel, axis, size), out_shape=...  34.6 us
    dot_general x3, matrix products, matmul(): return jnp.dot(left, right, preferred_element_type=jnp.float32)  25.5 us
    dot_general x3, matrix products, matmul_nt(): lax.dot_general(left, right, (((1,), (1,)), ((), ())), preferred_element_...  21.6 us
    dot_general x6, matrix products, matmul_tn(): lax.dot_general(left, right, (((0,), (0,)), ((), ())), preferred_element_...  19.4 us
  transfers between devices with their start and end apart: 6, of which 3 were waited for; matrix products, arithmetic and copies ran while one was open for 22% of the time, Pallas kernels for 48%

profile of v1, /device:TPU:0, one launch (start us, length us, event | category | flops | bytes accessed | tf_op | source)
XLA Modules:
  0.0 387.6 jit_solution(11290324531861203468)
XLA Ops:
  16.2 3.0 multiply_sine_fusion
  19.2 90.8 %attn_front_10.1 = (f32[128,1152]{1,0:T(8,128)}, f32[128,1152]{1,0:T(8,128)}, f32[128,1024]{1,0:T(8,128)}, f32[128,256]{1,0:T(8,128)}, bf16[128,1024]{1,0:T(8,12...) custom-call(bf16[128,1152]{1,0:T(8,128)(2,1)} %tokens.3, ...), custom_call_target="tpu_custom_call" | custom-call | bytes 117964800 | tf_op jit(solution)/shard_map/attn_front_10/pallas_call | solution.py:1048
  111.5 6.8 %fusion.14 = f32[1024,864]{0,1:T(8,128)} fusion(bf16[1024,1152]{1,0:T(8,128)(2,1)} %bitcast.66, bf16[1152,864]{1,0:T(8,128)(2,1)} %all-gather.4.cloned.1.call-done), kind=kOutput, calls=%fused_computation.65 | convolution fusion | flops 2038431744 | bytes 7888896 | tf_op jit(solution)/shard_map/dot_general | solution.py:69
  118.2 3.6 all-gather.6.cloned.1.call-done
  121.8 8.3 %multiply_convert_fusion.1 = (bf16[1024,864]{0,1:T(8,128)(2,1)}, f32[1024,864]{0,1:T(8,128)}) fusion(f32[1024,864]{0,1:T(8,128)} %fusion.14, bf16[1024,1152]{1,0:T(8,128)(2,1)S(1)} %bitcast.67, bf16[1152,864]{1,0:T(8,128)(2,1)} %all-gather.6.cloned.1.call-done), kind=kOutput, calls=%fused_computation.15 | convolution fusion | flops 2047279104 | bytes 13197312 | tf_op jit(solution)/shard_map/dot_general | solution.py:69
  130.1 37.2 %all-gather.8.cloned.1.call-done = bf16[1152,864]{1,0:T(8,128)(2,1)} async-done(((bf16[288,864]{1,0:T(8,128)(2,1)}), bf16[1152,864]{1,0:T(8,128)(2,1)}) %all-gather.8.cloned.1.call-update) | async-done | bytes 1990672 | tf_op jit(solution)/shard_map/all_gather | solution.py:1265
  167.4 6.4 %convolution_convert_fusion = bf16[1024,1152]{1,0:T(8,128)(2,1)} fusion(bf16[1024,864]{0,1:T(8,128)(2,1)} %get-tuple-element.124, bf16[1152,864]{1,0:T(8,128)(2,1)} %all-gather.8.cloned.1.call-done), kind=kOutput, calls=%fused_computation.3 | convolution fusion | flops 2039611392 | bytes 6119424 | tf_op jit(solution)/shard_map/dot_general | solution.py:79
  173.8 34.6 %ffn_turn_3.1 = (bf16[128,1152]{1,0:T(8,128)(2,1)}, f32[1,1152]{1,0:T(1,128)}, bf16[8,128,1152]{2,1,0:T(8,128)(2,1)}) custom-call(bf16[8,128,1152]{2,1,0:T(8,128)(2,1)} %bitcast.61, f32[128,1152]{1,0:T(8,128)} %get-tuple-element.54.residual, bf16[128,1152]{1,0:T(8,128)(2,1)} %cot.3, f32[1,1152]{1,0:T(1,128)} %slice.63.gain), custom_call_target="tpu_custom_call" | custom-call | bytes 47185920 | tf_op jit(solution)/shard_map/ffn_turn_3/pallas_call | solution.py:445
  208.4 6.2 %convolution_convert_fusion.3 = bf16[1152,864]{1,0:T(8,128)(2,1)} fusion(bf16[1024,1152]{1,0:T(8,128)(2,1)} %bitcast.70, bf16[1024,864]{0,1:T(8,128)(2,1)} %get-tuple-element.124), kind=kOutput, calls=%fused_computation.6 | convolution fusion | flops 2039427072 | bytes 6119424 | tf_op jit(solution)/shard_map/dot_general | solution.py:73
  214.7 10.4 %multiply_convert_fusion = (bf16[1024,864]{0,1:T(8,128)(2,1)}, bf16[1024,864]{0,1:T(8,128)(2,1)S(1)}) fusion(f32[1024,864]{0,1:T(8,128)} %fusion.14, f32[1024,864]{0,1:T(8,128)} %get-tuple-element.125, bf16[1024,1152]{1,0:T(8,128)(2,1)} %bitcast.71, bf16[1152,864]{1,0:T(8,128)(2,1)} %all-gather.8.cloned.1.call-done), kind=kOutput, calls=%fused_computation.14 | convolution fusion | flops 2058780672 | bytes 14966784 | tf_op jit(solution)/shard_map/dot_general | solution.py:69
  226.3 4.0 %convolution_convert_fusion.1 = bf16[1152,864]{1,0:T(8,128)(2,1)} fusion(bf16[1024,1152]{1,0:T(8,128)(2,1)S(1)} %bitcast.68, bf16[1024,864]{0,1:T(8,128)(2,1)S(1)} %get-tuple-element.117), kind=kOutput, calls=%fused_computation.4 | convolution fusion | flops 2039427072 | bytes 6119424 | tf_op jit(solution)/shard_map/dot_general | solution.py:73
  230.6 7.3 %fusion.15 = f32[1024,1152]{1,0:T(8,128)} fusion(bf16[1024,864]{0,1:T(8,128)(2,1)} %copy-done.10, bf16[1152,864]{1,0:T(8,128)(2,1)} %all-gather.4.cloned.1.call-done), kind=kOutput, calls=%fused_computation.66 | convolution fusion | flops 2038431744 | bytes 8478720 | tf_op jit(solution)/shard_map/dot_general | solution.py:79
  237.9 4.0 %convolution_convert_fusion.2 = bf16[1152,864]{1,0:T(8,128)(2,1)} fusion(bf16[1024,1152]{1,0:T(8,128)(2,1)S(1)} %bitcast.69, bf16[1024,864]{0,1:T(8,128)(2,1)S(1)} %copy-done.11), kind=kOutput, calls=%fused_computation.5 | convolution fusion | flops 2039427072 | bytes 6119424 | tf_op jit(solution)/shard_map/dot_general | solution.py:73
  241.9 7.9 %add_convert_fusion = bf16[1024,1152]{1,0:T(8,128)(2,1)} fusion(f32[1024,1152]{1,0:T(8,128)} %fusion.15, bf16[1024,864]{0,1:T(8,128)(2,1)} %get-tuple-element.116, bf16[1152,864]{1,0:T(8,128)(2,1)} %all-gather.6.cloned.1.call-done), kind=kOutput, calls=%fused_computation.2 | convolution fusion | flops 2040791040 | bytes 10838016 | tf_op jit(solution)/shard_map/dot_general | solution.py:79
  249.8 46.9 %attn_back_5.1 = (f32[128,1152]{1,0:T(8,128)}, bf16[8,128,128]{2,1,0:T(8,128)(2,1)}, bf16[8,128,64]{2,1,0:T(8,128)(2,1)}, bf16[8,128,144]{2,1,0:T(8,128)(2,1)}, f32[8,8,1152]{2,1,0:T(8,128)}) custom-call(bf16[8,128,1152]{2,1,0:T(8,128)(2,1)} %bitcast.62, f32[128,1152]{1,0:T(8,128)} %get-tuple-element.54.residual, bf16[128,1152]{1,0:T(8,128)(2,1)} %cot.3, ...), custom_call_target="tpu_custom_call" | custom-call | bytes 70778880 | tf_op jit(solution)/shard_map/attn_back_5/pallas_call | solution.py:709
  301.4 2.2 fusion.9
  304.5 1.5 fusion.7
  306.1 28.9 %exchange_8.1 = (bf16[4,288,128]{2,1,0:T(8,128)(2,1)}, bf16[4,288,64]{2,1,0:T(8,128)(2,1)}, bf16[4,256,144]{2,1,0:T(8,128)(2,1)}, f32[4,1,1280]{2,1,0:T(1,128)}) custom-call(bf16[4,288,128]{2,1,0:T(8,128)(2,1)} %bitcast.64, bf16[4,288,64]{2,1,0:T(8,128)(2,1)} %bitcast.65, bf16[4,256,144]{2,1,0:T(8,128)(2,1)} %bitcast.63, f32[4,1,1280]{2,1,0:T(1,128)} %broadcast_in_dim.19.refs_3_), custom_call_target="tpu_custom_call" | custom-call | bytes 15155200 | tf_op jit(solution)/shard_map/exchange_8/pallas_call | solution.py:222
  335.9 1.7 reduce_sum.59.refs_0_
  339.0 18.1 %exchange_9.1 = (bf16[8,288,128]{2,1,0:T(8,128)(2,1)}, bf16[8,288,64]{2,1,0:T(8,128)(2,1)}, bf16[8,256,144]{2,1,0:T(8,128)(2,1)}) custom-call(bf16[288,128]{1,0:T(8,128)(2,1)} %reduce_sum.59.refs_0_, bf16[288,64]{1,0:T(8,128)(2,1)} %reduce_sum.60.refs_1_, bf16[256,144]{1,0:T(8,128)(2,1)} %reduce_sum.61.refs_2_), custom_call_target="tpu_custom_call" | custom-call | bytes 29491200 | tf_op jit(solution)/shard_map/exchange_9/pallas_call | solution.py:222
  365.4 2.1 convert_element_type.139
  367.5 2.1 convert_element_type.137
  369.6 7.3 %reduce-scatter.6.cloned.1.call-done = bf16[288,864]{1,0:T(8,128)(2,1)} async-done(((bf16[1152,864]{1,0:T(8,128)(2,1)}), bf16[288,864]{1,0:T(8,128)(2,1)}) %reduce-scatter.6.cloned.1.call-update) | async-done | bytes 497680 | tf_op jit(solution)/shard_map/reduce_scatter | solution.py:1383
  376.9 2.1 convert_element_type.138
  (93 shorter events, 29.5 us)
Async XLA Ops:
  7.2 104.3 %all-gather.4.cloned.1.call-start = ((), (), s32[]{:S(2)}) async-start(), calls=%async_computation.3 | async-start | bytes 2580480 | tf_op jit(solution)/shard_map/all_gather | solution.py:1263
  7.9 113.9 %all-gather.6.cloned.1.call-start = ((), (), s32[]{:S(2)}) async-start(), calls=%async_computation.4 | async-start | bytes 2580480 | tf_op jit(solution)/shard_map/all_gather | solution.py:1264
  8.7 158.7 %all-gather.8.cloned.1.call-start = ((), (), s32[]{:S(2)}) async-start(), calls=%async_computation.5 | async-start | bytes 2580480 | tf_op jit(solution)/shard_map/all_gather | solution.py:1265
  9.4 356.0 %reduce-scatter.8.cloned.1.call-start = ((), (), s32[]{:S(2)}) async-start(), calls=%async_computation.8 | async-start | bytes 2580480 | tf_op jit(solution)/shard_map/reduce_scatter | solution.py:1323
  111.4 10.4 %copy-start.8 = (bf16[8,128,1152]{2,1,0:T(8,128)(2,1)S(1)}, bf16[8,128,1152]{2,1,0:T(8,128)(2,1)}, u32[]{:S(2)}) copy-start(bf16[8,128,1152]{2,1,0:T(8,128)(2,1)} %get-tuple-element.53) | copy-start | bytes 7077892
  214.6 152.9 %reduce-scatter.4.cloned.1.call-start = ((), (), s32[]{:S(2)}) async-start(), calls=%async_computation.6 | async-start | bytes 2580480 | tf_op jit(solution)/shard_map/reduce_scatter | solution.py:1330
  225.1 1.2 copy-start.10
  230.4 146.5 %reduce-scatter.6.cloned.1.call-start = ((), (), s32[]{:S(2)}) async-start(), calls=%async_computation.7 | async-start | bytes 2580480 | tf_op jit(solution)/shard_map/reduce_scatter | solution.py:1383
  230.6 7.3 %copy-start.11 = (bf16[1024,864]{0,1:T(8,128)(2,1)S(1)}, bf16[1024,864]{0,1:T(8,128)(2,1)}, u32[]{:S(2)}) copy-start(bf16[1024,864]{0,1:T(8,128)(2,1)} %get-tuple-element.116) | copy-start | bytes 5308420
  249.8 49.2 %copy-start = (bf16[8,128,1152]{2,1,0:T(8,128)(2,1)S(1)}, bf16[8,128,1152]{2,1,0:T(8,128)(2,1)}, u32[]{:S(2)}) copy-start(bf16[8,128,1152]{2,1,0:T(8,128)(2,1)} %get-tuple-element.72) | copy-start | bytes 7077892
  298.2 3.2 copy-start.9
  301.4 3.2 copy-start.7
  335.0 2.5 copy-start.6
  335.0 3.2 copy-start.4
  358.3 2.2 copy-start.1
  361.6 2.7 copy-start.2
  365.4 13.6 %copy-start.5 = (bf16[128,1152]{1,0:T(8,128)(2,1)S(1)}, bf16[128,1152]{1,0:T(8,128)(2,1)}, u32[]{:S(2)}) copy-start(bf16[128,1152]{1,0:T(8,128)(2,1)} %get-tuple-element.147) | copy-start | bytes 884740
  365.4 14.3 %copy-start.3 = (f32[128,1152]{1,0:T(8,128)S(1)}, f32[128,1152]{1,0:T(8,128)}, u32[]{:S(2)}) copy-start(f32[128,1152]{1,0:T(8,128)} %get-tuple-element.148) | copy-start | bytes 1769476
Sparse Core Ops, SparseCore 0:
  9.6 66.8 all-gather.3
  78.0 43.7 all-gather.5
  123.4 43.9 all-gather.7
  214.8 42.4 reduce-scatter.7
  259.4 42.3 reduce-scatter.3
  335.2 41.6 reduce-scatter.5
